TPU v7x, 32 devices: a whole 2x2x4 slice. The times are simulated.
32 devices in a mesh: groups: 2 (over y), feat: 4 (over z), rows: 2 (over x), sub: 2 (over core).
Axes of the slice: x: 2, y: 2, z: 4, core: 2. Of those that a mesh axis runs over, the one named last changes fastest.
Arguments:
- activations: bfloat16 [8192, 28672], P(('groups', 'rows', 'sub'), 'feat'), parts along dimension 0, may hold values from -6 to 6
- out_grads: bfloat16 [8192, 8192], P(('groups', 'rows', 'sub'), 'feat'), parts along dimension 0, may hold values from -6 to 6
- proj_in: bfloat16 [57344, 128], P(('groups', 'feat')), parts along dimension 0, may hold values from -0.03125 to 0.03125
- proj_out: bfloat16 [16384, 128], P(('groups', 'feat')), parts along dimension 0, may hold values from -0.0625 to 0.0625
- lengths: int32 [256], P('groups'), parts along dimension 0, may hold values from 1 to 64, 4096 in all
- corpus: bfloat16 [16384, 16384], P(('groups', 'rows', 'sub'), 'feat'), parts along dimension 0, may hold values from -200 to 200
- owner: int32 [8192], P(('rows', 'sub')), may hold values from 0 to 255, as said below
Outputs:
- influence: float32 [256, 16384], P(('groups', 'rows', 'sub'), 'feat'), parts along dimension 0
There are 2 independent parts, one for each index of `groups`. A program takes and returns all parts, laid end to end along the dimension named above; an argument that names none is the same for every part. Nothing has to cross between parts.
Inputs may be any that keep to these rules, and one draw needn't show every extreme that they name: `owner`: every draw holds at least two different labels, so each passage keeps some corpus rows.
All inputs are finite; a program needn't handle non-finite values.
Results may differ from a plain program's by a relative error of at most 0.007.
The roundings to bfloat16 on the way count: a program that leaves them out, or rounds other values in their place, can miss the bound.
Values may be sent and summed in bfloat16 or wider, within the bound.
A program may use at most 128 MiB of HBM per device.

v0:
```python
import math

import jax
import jax.numpy as jnp
from jax import lax
from jax.sharding import PartitionSpec as P

K = 16384


def local(activations, out_grads, proj_in, proj_out, lengths, corpus, owner):
    tok_local = activations.shape[0]
    passages = lengths.shape[0]
    nfeat = lax.axis_size("feat")
    part_x = jnp.dot(activations, proj_in, preferred_element_type=jnp.float32)
    part_g = jnp.dot(out_grads, proj_out, preferred_element_type=jnp.float32)
    width_cols = part_g.shape[1] // nfeat
    summed_x = lax.psum(part_x, "feat")
    x_low = summed_x.astype(jnp.bfloat16)
    g_low = lax.psum_scatter(part_g, "feat", scatter_dimension=1, tiled=True).astype(jnp.bfloat16)
    ends = jnp.cumsum(lengths)
    starts = ends - lengths
    positions = lax.axis_index(("rows", "sub")) * tok_local + jnp.arange(tok_local, dtype=jnp.int32)
    member = (
        (positions[None, :] >= starts[:, None]) & (positions[None, :] < ends[:, None])
    ).astype(jnp.bfloat16)
    scaled_member = member[None, :, :] * jnp.transpose(g_low)[:, None, :]
    partial_grad = jnp.einsum(
        "apt,tb->pab", scaled_member, x_low, preferred_element_type=jnp.float32
    )
    partial_grad = partial_grad.reshape(passages, width_cols * x_low.shape[1])
    pgrad = lax.psum(partial_grad, ("rows", "sub"))
    pgrad_low = pgrad.astype(jnp.bfloat16)
    sumsq_part = jnp.sum(pgrad * pgrad, axis=1)
    raw_part = lax.dot_general(
        pgrad_low, corpus, (((1,), (1,)), ((), ())), preferred_element_type=jnp.float32
    )
    labels = jnp.arange(passages, dtype=jnp.int32)[:, None]
    raw, sumsq = lax.psum((raw_part, sumsq_part), "feat")
    scale = 2.5 / math.sqrt(K) * lax.rsqrt(sumsq / K + 1e-06)
    score = raw * scale[:, None]
    owned = owner[None, :] == labels
    local_top = jnp.max(jnp.where(owned, jnp.float32(-1e30), score), axis=1)
    top = lax.pmax(local_top, ("rows", "sub"))
    weight = jnp.where(owned, jnp.float32(0.0), jnp.exp(score - top[:, None]))
    total = lax.psum(jnp.sum(weight, axis=1), ("rows", "sub"))
    weight_low = weight.astype(jnp.bfloat16)
    span = passages // lax.axis_size(("rows", "sub"))
    summed = lax.psum_scatter(
        jnp.dot(weight_low, corpus, preferred_element_type=jnp.float32),
        ("rows", "sub"),
        scatter_dimension=0,
        tiled=True,
    )
    own_total = lax.dynamic_slice_in_dim(total, lax.axis_index(("rows", "sub")) * span, span, 0)
    return summed / own_total[:, None]


def solution(mesh):
    return jax.shard_map(
        local,
        mesh=mesh,
        in_specs=(
            P(("groups", "rows", "sub"), "feat"),
            P(("groups", "rows", "sub"), "feat"),
            P(("groups", "feat"), None),
            P(("groups", "feat"), None),
            P("groups"),
            P(("groups", "rows", "sub"), "feat"),
            P(("rows", "sub")),
        ),
        out_specs=P(("groups", "rows", "sub"), "feat"),
        check_vma=False,
    )
```

profile of v0, /device:TPU:0, one launch (start us, length us, event | category | flops | bytes accessed | tf_op | source)
XLA Modules:
  0.0 233.4 jit_solution(10716244795493063472)
XLA Ops:
  6.5 4.7 %fusion.18 = f32[1024,128]{0,1:T(8,128)} fusion(bf16[1024,2048]{1,0:T(8,128)(2,1)} %param.8, bf16[2048,128]{1,0:T(8,128)(2,1)} %param.10), kind=kOutput, calls=%fused_computation.26 | convolution fusion | flops 536870912 | bytes 5242880 | tf_op jit(solution)/shard_map/dot_general | solution.py:16
  11.3 0.0 reduce-scatter.3.cloned.1.call-update
  11.3 0.0 copy-start.3
  11.3 0.0 all-reduce.4.cloned.1.call-start
  11.4 10.1 %fusion.17 = f32[1024,128]{0,1:T(8,128)S(1)} fusion(bf16[1024,7168]{1,0:T(8,128)(2,1)} %param.7, bf16[7168,128]{1,0:T(8,128)(2,1)S(1)} %copy-done), kind=kOutput, calls=%fused_computation.25 | convolution fusion | flops 1879048192 | bytes 17039360 | tf_op jit(solution)/shard_map/dot_general | solution.py:15
  21.5 0.1 copy.9
  21.7 0.2 reduce-window.8
  21.8 0.1 reduce
  22.0 0.1 and_convert_fusion
  22.1 34.1 %all-reduce.7 = bf16[1024,128]{0,1:T(8,128)(2,1)S(1)} all-reduce(f32[1024,128]{0,1:T(8,128)S(1)} %fusion.17), channel_id=1, replica_groups=mesh['groups'=2,'feat'=4,'rows'=2,'sub'=2] {'feat'}, use_global_device_ids=true, to_apply=%region_0.0 | all-reduce | flops 131072 | bytes 786432 | tf_op jit(solution)/shard_map/psum | solution.py:18
  56.3 0.0 reduce-scatter.3.cloned.1.call-done
  56.3 0.9 convert_bitcast_fusion
  57.2 4.1 %fusion = f32[128,32,128]{2,0,1:T(8,128)} fusion(bf16[32,1024]{1,0:T(8,128)(2,1)S(1)} %convert_bitcast_fusion, bf16[128,1024]{1,0:T(8,128)(2,1)S(1)} %and_convert_fusion, bf16[1024,128]{0,1:T(8,128)(2,1)S(1)} %all-reduce.7), kind=kOutput, calls=%fused_computation | convolution fusion | flops 1090519040 | bytes 2686976 | tf_op jit(solution)/shard_map/apt,tb->pab/dot_general | solution.py:28
  61.3 0.0 all-reduce.4.cloned.1.call-update
  61.4 0.0 copy-start.2
  61.4 0.0 all-reduce.6.cloned.1.call-start
  61.4 49.9 %all-reduce.4.cloned.1.call-done = f32[128,4096]{0,1:T(8,128)} async-done(((f32[128,4096]{0,1:T(8,128)}), f32[128,4096]{0,1:T(8,128)}) %all-reduce.4.cloned.1.call-update) | async-done | bytes 2097168 | tf_op jit(solution)/shard_map/psum | solution.py:32
  111.3 13.1 %fusion.4 = f32[128,2048]{1,0:T(8,128)} fusion(bf16[2048,4096]{1,0:T(8,128)(2,1)} %param.12, f32[128,4096]{0,1:T(8,128)} %all-reduce.4.cloned.1.call-done), kind=kOutput, calls=%fused_computation.7 | convolution fusion | flops 2148007936 | bytes 19922944 | tf_op jit(solution)/shard_map/dot_general | solution.py:35
  124.4 0.0 all-reduce.6.cloned.1.call-update
  124.4 0.0 reduce-scatter.5.cloned.1.call-start
  124.5 2.1 multiply_reduce_fusion
  126.6 12.1 %psum.38 = f32[128]{0:T(128)S(1)} all-reduce(f32[128]{0:T(128)S(1)} %multiply_reduce_fusion), channel_id=1, replica_groups=mesh['groups'=2,'feat'=4,'rows'=2,'sub'=2] {'feat'}, use_global_device_ids=true, to_apply=%region_6.7 | all-reduce | flops 128 | bytes 1024 | tf_op jit(solution)/shard_map/psum | solution.py:39
  138.7 37.9 %all-reduce.6.cloned.1.call-done = f32[128,2048]{1,0:T(8,128)} async-done(((f32[128,2048]{1,0:T(8,128)}), f32[128,2048]{1,0:T(8,128)}) %all-reduce.6.cloned.1.call-update) | async-done | bytes 1048592 | tf_op jit(solution)/shard_map/psum | solution.py:39
  176.6 1.5 select_reduce_fusion
  178.2 7.0 %pmax.7 = f32[128]{0:T(128)S(1)} all-reduce(f32[128]{0:T(128)S(1)} %select_reduce_fusion), channel_id=1, replica_groups=mesh['groups'=2,'feat'=4,'rows'=2,'sub'=2] {'rows','sub'}, use_global_device_ids=true, to_apply=%region_8.9 | all-reduce | flops 128 | bytes 1024 | tf_op jit(solution)/shard_map/pmax | solution.py:44
  185.2 10.0 %fusion.8 = f32[128,4096]{1,0:T(8,128)} fusion(bf16[2048,4096]{1,0:T(8,128)(2,1)} %param.12, f32[128,2048]{1,0:T(8,128)} %all-reduce.6.cloned.1.call-done, f32[128]{0:T(128)S(1)} %pmax.7, f32[128]{0:T(128)S(1)} %rsqrt_multiply_fusion, s32[2048]{0:T(1024)S(1)} %copy-done.2), kind=kOutput, calls=%fused_computation.12 | convolution fusion | flops 2148794368 | bytes 19932160 | tf_op jit(solution)/shard_map/dot_general | solution.py:50
  195.2 0.0 reduce-scatter.5.cloned.1.call-update
  195.3 0.4 fusion.6
  195.6 5.9 %psum.39 = f32[128]{0:T(128)S(1)} all-reduce(f32[128]{0:T(128)S(1)} %fusion.6), channel_id=1, replica_groups=mesh['groups'=2,'feat'=4,'rows'=2,'sub'=2] {'rows','sub'}, use_global_device_ids=true, to_apply=%region_11.12 | all-reduce | flops 128 | bytes 1024 | tf_op jit(solution)/shard_map/psum | solution.py:46
  201.6 0.1 dynamic_slice.3
  201.7 23.3 %reduce-scatter.5.cloned.1.call-done = f32[32,4096]{1,0:T(8,128)} async-done(((f32[128,4096]{1,0:T(8,128)}), f32[32,4096]{1,0:T(8,128)}) %reduce-scatter.5.cloned.1.call-update) | async-done | bytes 524304 | tf_op jit(solution)/shard_map/reduce_scatter | solution.py:49
  224.9 1.9 broadcast_divide_fusion
  (10 shorter events, 0.0 us)
Async XLA Ops:
  6.5 4.8 %copy-start = (bf16[7168,128]{1,0:T(8,128)(2,1)S(1)}, bf16[7168,128]{1,0:T(8,128)(2,1)}, u32[]{:S(2)}) copy-start(bf16[7168,128]{1,0:T(8,128)(2,1)} %param.9) | copy-start | bytes 5505028
  6.5 49.8 %reduce-scatter.3.cloned.1.call-start = ((), (), s32[]{:S(2)}) async-start(), calls=%async_computation.2 | async-start | bytes 655360 | tf_op jit(solution)/shard_map/reduce_scatter | solution.py:20
  11.3 10.2 %copy-start.3 = (s32[128]{0:T(128)S(1)}, s32[128]{0:T(128)}, u32[]{:S(2)}) copy-start(s32[128]{0:T(128)} %param.11) | copy-start | bytes 1540
  11.3 100.0 %all-reduce.4.cloned.1.call-start = ((), (), s32[]{:S(2)}) async-start(), calls=%async_computation.3 | async-start | bytes 4194304 | tf_op jit(solution)/shard_map/psum | solution.py:32
  61.4 115.3 %copy-start.2 = (s32[2048]{0:T(1024)S(1)}, s32[2048]{0:T(1024)}, u32[]{:S(2)}) copy-start(s32[2048]{0:T(1024)} %param.13) | copy-start | bytes 24580
  61.4 115.3 %all-reduce.6.cloned.1.call-start = ((), (), s32[]{:S(2)}) async-start(), calls=%async_computation.4 | async-start | bytes 2097152 | tf_op jit(solution)/shard_map/psum | solution.py:39
  124.4 100.5 %reduce-scatter.5.cloned.1.call-start = ((), (), s32[]{:S(2)}) async-start(), calls=%async_computation.5 | async-start | bytes 2621440 | tf_op jit(solution)/shard_map/reduce_scatter | solution.py:49
  185.2 10.0 %copy-start.1 = (f32[128,2048]{1,0:T(8,128)S(1)}, f32[128,2048]{1,0:T(8,128)}, u32[]{:S(2)}) copy-start(f32[128,2048]{1,0:T(8,128)} %all-reduce.6.cloned.1.call-done) | copy-start | bytes 3145732
Sparse Core Ops, SparseCore 0:
  11.4 26.4 reduce-scatter.2
  61.5 49.7 all-reduce.3
  124.5 52.0 all-reduce.5
  195.4 29.5 reduce-scatter.4
where the time goes:
time: 234 us; the launch traced here: 233 us
  waiting for transfers between devices  111 us (47%)
  blocking collectives  59.2 us (25%)
  matrix products  42.1 us (18%)
  between operations  13.2 us (6%)
  other arithmetic  7.37 us (3%)
    psum x1, waiting for transfers between devices, local(): pgrad = lax.psum(partial_grad, ('rows', 'sub'))  49.9 us
    psum x1, waiting for transfers between devices, local(): raw, sumsq = lax.psum((raw_part, sumsq_part), 'feat')  37.9 us
    psum x1, blocking collectives, local(): summed_x = lax.psum(part_x, 'feat')  34.1 us
    reduce_scatter x1, waiting for transfers between devices, local(): lax.psum_scatter(jnp.dot(weight_low, corpus, preferred_element_type=jnp.f...  23.3 us
    dot_general x1, matrix products, local(): lax.dot_general(pgrad_low, corpus, (((1,), (1,)), ((), ())), preferred_el...  13.1 us
    psum x1, blocking collectives, local(): raw, sumsq = lax.psum((raw_part, sumsq_part), 'feat')  12.1 us
    dot_general x1, matrix products, local(): part_x = jnp.dot(activations, proj_in, preferred_element_type=jnp.float32)  10.1 us
    dot_general x1, matrix products, local(): jnp.dot(weight_low, corpus, preferred_element_type=jnp.float32)  10 us
  transfers between devices with their start and end apart: 4, of which 3 were waited for; matrix products, arithmetic and copies ran while one was open for 6% of the time, Pallas kernels for 0%

commit v1 on v0

v1 whole, which is shorter than its diff:
```python
import functools
import math

import jax
import jax.numpy as jnp
from jax import lax
from jax.experimental import pallas as pl
from jax.experimental.pallas import tpu as pltpu
from jax.sharding import PartitionSpec as P

MESH = pl.DeviceIdType.MESH
F32 = jnp.float32
BF16 = jnp.bfloat16
NT = (((1,), (1,)), ((), ()))
WINDOW = 256


def remote(src, dst, send, recv, target):
    return pltpu.make_async_remote_copy(
        src_ref=src, dst_ref=dst, send_sem=send, recv_sem=recv,
        device_id=target, device_id_type=MESH)


def kernel(nz, nx, ns, win, act, og, pin, pout, owner, corpus, out,
           act_v, og_v, pin_v, pout_v, cor_v,
           g_send, g_recv, x_send, x_recv, x_all, gt_all, x_blk, g_blk, pgf, pg_low, sq,
           raw_send, raw_recv, w_all, st_x, st_s, fac,
           dbuf, dpart, d2, d3,
           ld, ldc, gs, gr, xs, xr, xzs, xzr, gis, gir, xis, xir, fws, fwr,
           rs, rr, ws, wr, fs, fr, sxs, sxr, sss, ssr, d1s, d1r, d2s, d2r):
    mz, mx, ms = lax.axis_index("feat"), lax.axis_index("rows"), lax.axis_index("sub")
    tok, _ = act.shape
    ni = nx * ns
    total_tok = tok * ni
    passages = win.shape[1]
    rank = pin.shape[1]
    cols = rank // nz
    tc = tok // nz
    rows, kc = corpus.shape
    pcz = passages // nz
    pci = passages // ni
    nb, rb = raw_send.shape[0], raw_send.shape[3] - 128
    ncb, cb = dbuf.shape[0], dbuf.shape[3]
    k_total = rank * rank
    os = lax.rem(ms + 1, ns)
    mi = mx * ns + ms

    def zp(o):
        return lax.rem(mz + o, nz)

    def xp(o):
        return lax.rem(mx + o, nx)

    c_og = pltpu.make_async_copy(og, og_v, ld.at[0])
    c_po = pltpu.make_async_copy(pout, pout_v, ld.at[1])
    c_pi = pltpu.make_async_copy(pin, pin_v, ld.at[2])
    c_po.start()
    c_og.start()
    c_pi.start()
    c_act = []
    for o in range(1, nz + 1):
        d = zp(o)
        at = pl.ds(pl.multiple_of(d * tc, tc), tc)
        c_act.append(pltpu.make_async_copy(act.at[at], act_v.at[at], ld.at[2 + o]))
        c_act[-1].start()
    c_cor = []
    for b in range(nb):
        at = pl.ds(b * rb, rb)
        c_cor.append(pltpu.make_async_copy(corpus.at[at], cor_v.at[at], ldc.at[b]))

    barrier = pltpu.get_barrier_semaphore()
    for o in range(1, nz):
        pl.semaphore_signal(barrier, inc=1, device_id={"feat": zp(o)}, device_id_type=MESH)
    for o in range(1, nx):
        pl.semaphore_signal(barrier, inc=1, device_id={"rows": xp(o)}, device_id_type=MESH)
    pl.semaphore_signal(barrier, inc=1, device_id={"sub": os}, device_id_type=MESH)
    pl.semaphore_wait(barrier, nz - 1 + nx - 1 + 1)

    c_po.wait()
    c_og.wait()
    g_t = jnp.transpose(jnp.dot(og_v[...], pout_v[...], preferred_element_type=F32))
    for j in range(nz):
        g_send[j] = g_t[j * cols:(j + 1) * cols]
    g_copies = [remote(g_send.at[zp(o)], g_recv.at[mz], gs.at[o - 1], gr.at[mz], {"feat": zp(o)})
                for o in range(1, nz)]
    for c in g_copies:
        c.start()

    c_pi.wait()
    x_copies = []
    for o in range(1, nz + 1):
        d = zp(o)
        at = pl.ds(pl.multiple_of(d * tc, tc), tc)
        c_act[o - 1].wait()
        x_send[d] = jnp.dot(act_v[at], pin_v[...], preferred_element_type=F32)
        if o < nz:
            c = remote(x_send.at[d], x_recv.at[mz], xs.at[o - 1], xr.at[mz], {"feat": d})
            c.start()
            x_copies.append(c)
        if o == max(1, nz // 2):
            for c in c_cor:
                c.start()

    def wait_recv(dst, sem, target):
        remote(dst, dst, sem, sem, target).wait_recv()

    g_sum = g_send[mz]
    for o in range(1, nz):
        s = zp(o)
        wait_recv(g_recv.at[s], gr.at[s], {"feat": s})
        g_sum = g_sum + g_recv[s]

    def tok_at(x, s):
        return pl.ds(pl.multiple_of((x * ns + s) * tok, tok), tok)

    mine = tok_at(mx, ms)
    gt_all[:, mine] = g_sum.astype(BF16)
    gi = []
    for o in range(1, nx):
        gi.append(remote(gt_all.at[:, mine], gt_all.at[:, mine], gis.at[o - 1], gir.at[mx], {"rows": xp(o)}))
    gi.append(remote(gt_all.at[:, mine], gt_all.at[:, mine], gis.at[nx - 1], fwr.at[0, mx], {"sub": os}))
    for c in gi:
        c.start()

    x_sum = x_send[mz]
    for o in range(1, nz):
        s = zp(o)
        wait_recv(x_recv.at[s], xr.at[s], {"feat": s})
        x_sum = x_sum + x_recv[s]

    def chunk_at(z):
        return pl.ds(pl.multiple_of((mi * nz + z) * tc, tc), tc)

    own = chunk_at(mz)
    x_all[own] = x_sum.astype(BF16)
    xz = [remote(x_all.at[own], x_all.at[own], xzs.at[o - 1], xzr.at[mz], {"feat": zp(o)}) for o in range(1, nz)]
    for c in xz:
        c.start()

    fw = []
    for o in range(1, nx):
        s = xp(o)
        at = tok_at(s, ms)
        wait_recv(gt_all.at[:, at], gir.at[s], {"rows": s})
        c = remote(gt_all.at[:, at], gt_all.at[:, at], fws.at[0, o - 1], fwr.at[0, s], {"sub": os})
        c.start()
        fw.append(c)

    for o in range(1, nz):
        s = zp(o)
        wait_recv(x_all.at[chunk_at(s)], xzr.at[s], {"feat": s})

    xi = []
    for o in range(1, nx):
        xi.append(remote(x_all.at[mine], x_all.at[mine], xis.at[o - 1], xir.at[mx], {"rows": xp(o)}))
    xi.append(remote(x_all.at[mine], x_all.at[mine], xis.at[nx - 1], fwr.at[1, mx], {"sub": os}))
    for c in xi:
        c.start()
    for o in range(1, nx):
        s = xp(o)
        at = tok_at(s, ms)
        wait_recv(x_all.at[at], xir.at[s], {"rows": s})
        c = remote(x_all.at[at], x_all.at[at], fws.at[1, o - 1], fwr.at[1, s], {"sub": os})
        c.start()
        fw.append(c)
    for x in range(nx):
        at = tok_at(x, os)
        wait_recv(gt_all.at[:, at], fwr.at[0, x], {"sub": os})
        wait_recv(x_all.at[at], fwr.at[1, x], {"sub": os})

    for i in range(total_tok // 128):
        g_blk[i] = gt_all[:, i * 128:(i + 1) * 128].astype(F32)
        x_blk[i] = x_all[i * 128:(i + 1) * 128, :]
    lane = lax.broadcasted_iota(jnp.int32, (cols, WINDOW), 1)

    def passage(p, carry):
        keep = (lane >= win[1, p]) & (lane < win[2, p])
        first = win[0, p]
        second = win[3, p]
        gw = jnp.concatenate([g_blk[first], g_blk[second]], axis=1)
        gw = jnp.where(keep, gw, 0.0).astype(BF16)
        xw = jnp.concatenate([x_blk[first], x_blk[second]], axis=0)
        res = jnp.dot(gw, xw, preferred_element_type=F32)
        pgf[pl.ds(p, cols, stride=passages), :] = res
        sq[pl.ds(p, 1), :] = jnp.sum(res * res, axis=0, keepdims=True)
        return carry

    lax.fori_loop(0, passages, passage, 0, unroll=8)
    for a in range(cols):
        pg_low[:, a * rank:(a + 1) * rank] = pgf[a * passages:(a + 1) * passages, :].astype(BF16)
    sumsq = jnp.sum(sq[...], axis=1, keepdims=True) + jnp.zeros((passages, 128), F32)

    for b in range(nb):
        c_cor[b].wait()

    def score_block(b, carry):
        at = pl.ds(pl.multiple_of(b * rb, rb), rb)
        raw = lax.dot_general(pg_low[...], cor_v[at, :], NT, preferred_element_type=F32)
        for j in range(nz):
            raw_send[b, j, :, :rb] = raw[j * pcz:(j + 1) * pcz]
            raw_send[b, j, :, rb:] = sumsq[j * pcz:(j + 1) * pcz]
        for o in range(1, nz):
            d = zp(o)
            remote(raw_send.at[b, d], raw_recv.at[b, mz], rs.at[b, o - 1], rr.at[b, mz], {"feat": d}).start()
        return carry

    lax.fori_loop(0, nb, score_block, 0)

    labels = mz * pcz + lax.broadcasted_iota(jnp.int32, (pcz, rb), 0)
    scores = []
    for b in range(nb):
        acc = raw_send[b, mz]
        for o in range(1, nz):
            s = zp(o)
            wait_recv(raw_recv.at[b, s], rr.at[b, s], {"feat": s})
            acc = acc + raw_recv[b, s]
        scale = 2.5 / math.sqrt(k_total) * lax.rsqrt(acc[:, rb:rb + 1] / k_total + 1e-06)
        owned = owner[:, b * rb:(b + 1) * rb] == labels
        scores.append((owned, acc[:, :rb] * scale))
    top = functools.reduce(jnp.maximum, [
        jnp.max(jnp.where(owned, F32(-1e30), s), axis=1, keepdims=True) for owned, s in scores])
    total = jnp.zeros((pcz, 1), F32)
    for b in range(nb):
        owned, s = scores[b]
        w = jnp.where(owned, F32(0.0), jnp.exp(s - top))
        total = total + jnp.sum(w, axis=1, keepdims=True)
        w_all[mz, :, b * rb:(b + 1) * rb] = w.astype(BF16)
    wz = [remote(w_all.at[mz], w_all.at[mz], ws.at[o - 1], wr.at[mz], {"feat": zp(o)}) for o in range(1, nz)]
    for c in wz:
        c.start()

    full = jnp.zeros((pcz, 128), F32)
    st_x[mx, 0] = top + full
    st_x[mx, 1] = total + full
    sx = [remote(st_x.at[mx], st_x.at[mx], sxs.at[o - 1], sxr.at[mx], {"rows": xp(o)}) for o in range(1, nx)]
    for c in sx:
        c.start()
    for o in range(1, nx):
        s = xp(o)
        wait_recv(st_x.at[s], sxr.at[s], {"rows": s})
    top_x = functools.reduce(jnp.maximum, [st_x[x, 0] for x in range(nx)])
    tot_x = functools.reduce(jnp.add, [jnp.exp(st_x[x, 0] - top_x) * st_x[x, 1] for x in range(nx)])
    st_s[ms, 0] = top_x
    st_s[ms, 1] = tot_x
    ss = remote(st_s.at[ms], st_s.at[ms], sss.at[0], ssr.at[0], {"sub": os})
    ss.start()
    wait_recv(st_s.at[os], ssr.at[0], {"sub": os})
    top_all = functools.reduce(jnp.maximum, [st_s[s, 0] for s in range(ns)])
    tot_all = functools.reduce(jnp.add, [jnp.exp(st_s[s, 0] - top_all) * st_s[s, 1] for s in range(ns)])
    fac[mz] = jnp.exp(st_x[mx, 0] - top_all) / tot_all
    fz = [remote(fac.at[mz], fac.at[mz], fs.at[o - 1], fr.at[mz], {"feat": zp(o)}) for o in range(1, nz)]
    for c in fz:
        c.start()
    for o in range(1, nz):
        s = zp(o)
        wait_recv(w_all.at[s], wr.at[s], {"feat": s})
    for o in range(1, nz):
        s = zp(o)
        wait_recv(fac.at[s], fr.at[s], {"feat": s})

    w_full = w_all[...].reshape(passages, rows)
    factor = fac[...].reshape(passages, 128)[:, :1]

    def sub_copy(b):
        return remote(dbuf.at[b, os], dpart.at[b], d1s.at[b], d1r.at[b], {"sub": os})

    def weighted(b, carry):
        at = pl.ds(pl.multiple_of(b * cb, cb), cb)
        part = jnp.dot(w_full, cor_v[:, at], preferred_element_type=F32) * factor
        part = part.astype(BF16)
        for x in range(nx):
            for s in range(ns):
                i = x * ns + s
                dbuf[b, s, x * pci:(x + 1) * pci, :] = part[i * pci:(i + 1) * pci]
        sub_copy(b).start()
        return carry

    def row_copy(b, o):
        return remote(d2.at[b, xp(o)], d3.at[b, mx], d2s.at[b, o - 1], d2r.at[b, mx], {"rows": xp(o)})

    def merge(b, carry):
        sub_copy(b).wait_recv()
        both = dbuf[b, ms].astype(F32) + dpart[b].astype(F32)
        for x in range(nx):
            d2[b, x] = both[x * pci:(x + 1) * pci].astype(BF16)
        for o in range(1, nx):
            row_copy(b, o).start()
        return carry

    weighted(0, 0)

    def step(b, carry):
        weighted(b, carry)
        return merge(b - 1, carry)

    lax.fori_loop(1, ncb, step, 0)
    merge(ncb - 1, 0)

    def finish(b, carry):
        acc = d2[b, mx].astype(F32)
        for o in range(1, nx):
            s = xp(o)
            wait_recv(d3.at[b, s], d2r.at[b, s], {"rows": s})
            acc = acc + d3[b, s].astype(F32)
        out[:, pl.ds(pl.multiple_of(b * cb, cb), cb)] = acc
        sub_copy(b).wait_send()
        for o in range(1, nx):
            row_copy(b, o).wait_send()
        for o in range(1, nz):
            pass
        return carry

    lax.fori_loop(0, ncb, finish, 0)

    for c in g_copies + x_copies + gi + xz + xi + fw + wz + sx + [ss] + fz:
        c.wait_send()
    for b in range(nb):
        for o in range(1, nz):
            remote(raw_send.at[b, zp(o)], raw_recv.at[b, mz], rs.at[b, o - 1], rr.at[b, mz],
                   {"feat": zp(o)}).wait_send()


def local(activations, out_grads, proj_in, proj_out, lengths, corpus, owner):
    nz, nx, ns = lax.axis_size("feat"), lax.axis_size("rows"), lax.axis_size("sub")
    tok, din = activations.shape
    dout = out_grads.shape[1]
    rank = proj_in.shape[1]
    passages = lengths.shape[0]
    rows, kc = corpus.shape
    cols = rank // nz
    ni = nx * ns
    pcz, pci, tc = passages // nz, passages // ni, tok // nz
    ends = jnp.cumsum(lengths)
    starts = ends - lengths
    base = jnp.minimum(starts // 128 * 128, tok * ni - WINDOW)
    win = jnp.stack([base // 128, starts - base, ends - base, base // 128 + 1])
    nb = 4
    rb = rows // nb
    cb = min(kc, 512)
    ncb = kc // cb
    V, D = pltpu.VMEM, pltpu.SemaphoreType.DMA
    scratch = [
        V((tok, din), BF16), V((tok, dout), BF16), V((din, rank), BF16), V((dout, rank), BF16),
        V((rows, kc), BF16),
        V((nz, cols, tok), F32), V((nz, cols, tok), F32),
        V((nz, tc, rank), F32), V((nz, tc, rank), F32),
        V((tok * ni, rank), BF16), V((cols, tok * ni), BF16),
        V((tok * ni // 128, 128, rank), BF16), V((tok * ni // 128, cols, 128), F32),
        V((cols * passages, rank), F32), V((passages, cols * rank), BF16), V((passages, rank), F32),
        V((nb, nz, pcz, rb + 128), F32), V((nb, nz, pcz, rb + 128), F32),
        V((nz, pcz, rows), BF16),
        V((nx, 2, pcz, 128), F32), V((ns, 2, pcz, 128), F32), V((nz, pcz, 128), F32),
        V((ncb, ns, nx * pci, cb), BF16), V((ncb, nx * pci, cb), BF16),
        V((ncb, nx, pci, cb), BF16), V((ncb, nx, pci, cb), BF16),
        D((nz + 3,)), D((nb,)),
        D((nz,)), D((nz,)), D((nz,)), D((nz,)), D((nz,)), D((nz,)),
        D((nx,)), D((nx,)), D((nx,)), D((nx,)), D((2, nx)), D((2, nx)),
        D((nb, nz)), D((nb, nz)), D((nz,)), D((nz,)), D((nz,)), D((nz,)),
        D((nx,)), D((nx,)), D((1,)), D((1,)),
        D((ncb,)), D((ncb,)), D((ncb, nx)), D((ncb, nx)),
    ]
    anyspace = pl.BlockSpec(memory_space=pl.ANY)
    vmem = pl.BlockSpec(memory_space=pltpu.VMEM)
    return pl.pallas_call(
        functools.partial(kernel, nz, nx, ns),
        out_shape=jax.ShapeDtypeStruct((pci, kc), F32),
        in_specs=[pl.BlockSpec(memory_space=pltpu.SMEM), anyspace, anyspace, anyspace, anyspace, vmem, anyspace],
        out_specs=vmem,
        scratch_shapes=scratch,
        compiler_params=pltpu.CompilerParams(
            collective_id=0, has_side_effects=True, vmem_limit_bytes=67043328),
    )(win, activations, out_grads, proj_in, proj_out, owner.reshape(1, rows), corpus)


def solution(mesh):
    return jax.shard_map(
        local,
        mesh=mesh,
        in_specs=(
            P(("groups", "rows", "sub"), "feat"),
            P(("groups", "rows", "sub"), "feat"),
            P(("groups", "feat"), None),
            P(("groups", "feat"), None),
            P("groups"),
            P(("groups", "rows", "sub"), "feat"),
            P(("rows", "sub")),
        ),
        out_specs=P(("groups", "rows", "sub"), "feat"),
        check_vma=False,
    )
```

time: 234 us -> 110 us (0.47)
  waiting for transfers between devices: 111 us -> 0 us
  Pallas kernels: 0 us -> 106 us
  blocking collectives: 59.2 us -> 0 us
  matrix products: 42.1 us -> 0 us
  between operations: 13.2 us -> 0.02 us
  other arithmetic: 7.37 us -> 1.55 us
  local copies, waits for them, and re-layouts: 0.21 us -> 2.63 us
    pallas_call x0 -> x1, Pallas kernels: none -> 106 us  [local(): pl.pallas_call(functools.partial(kernel, nz, nx, ns), out_shape=jax.Shape...]
    psum x2 -> x0, waiting for transfers between devices: 87.8 us -> none  [the longest x1 49.9 us: local(): pgrad = lax.psum(partial_grad, ('rows', 'sub'))]
    psum x3 -> x0, blocking collectives: 52.2 us -> none  [the longest x1 34.1 us: local(): summed_x = lax.psum(part_x, 'feat')]
    dot_general x5 -> x0, matrix products: 42.1 us -> none  [the longest x1 13.1 us: local(): lax.dot_general(pgrad_low, corpus, (((1,), (1,)), ((), ())), preferred_el...]
    reduce_scatter x2 -> x0, waiting for transfers between devices: 23.3 us -> none  [the longest x1 23.3 us: local(): lax.psum_scatter(jnp.dot(weight_low, corpus, preferred_element_type=jnp.f...]
    pmax x1 -> x0, blocking collectives: 7.02 us -> none  [local(): top = lax.pmax(local_top, ('rows', 'sub'))]
    reduce_sum x2 -> x0, other arithmetic: 2.54 us -> none  [the longest x1 2.15 us: local(): sumsq_part = jnp.sum(pgrad * pgrad, axis=1)]
  transfers between devices with their start and end apart: 4 -> 0, of which waited for: 3 -> 0; matrix products, arithmetic and copies ran while one was open for 6% -> 0% of each run, Pallas kernels for 0% -> 0%
where the time goes in v1:
time: 110 us
  Pallas kernels  106 us (96%)
  local copies, waits for them, and re-layouts  2.63 us (2%)
  other arithmetic  1.55 us (1%)
    pallas_call x1, Pallas kernels, local(): pl.pallas_call(functools.partial(kernel, nz, nx, ns), out_shape=jax.Shape...  106 us

profile of v1, /device:TPU:0, one launch (start us, length us, event | category | flops | bytes accessed | tf_op | source)
XLA Modules:
  0.0 110.1 jit_solution(7082889752474080536)
XLA Ops:
  0.0 0.8 copy.9
  0.8 0.2 reduce-window.9
  0.9 0.1 reduce
  1.0 0.7 subtract_bitcast_fusion.1
  1.7 0.6 pad_add_fusion.win
  2.3 105.9 %shard_map.73 = f32[32,4096]{1,0:T(8,128)} custom-call(s32[4,128]{1,0:T(4,128)} %pad_add_fusion.win, bf16[1024,7168]{1,0:T(8,128)(2,1)} %act.1, bf16[1024,2048]{1,0:T(8,128)(2,1)} %og.1, bf16[7168,128]{1,0:T(8,128)(2,1)} %pin.1, bf16[2048,128]{1,0:T(8,128)(2,1)} %pout.1, s32[1,2048]{1,0:T(1,128)} %bitcast.9, bf16[2048,4096]{1,0:T(8,128)(2,1)} %corpus.1), custom_call_target="tpu_custom_call" | custom-call | tf_op jit(solution)/shard_map/pallas_call | solution.py:364
  108.2 1.9 %copy.11 = f32[32,4096]{1,0:T(8,128)} copy(f32[32,4096]{1,0:T(8,128)} %shard_map.73) | data formatting | bytes 1048576
  (1 shorter events, 0.0 us)
